TPU v7x, 256 devices: a whole 4x4x8 slice. The times are simulated.
256 devices in a mesh: proj: 16 (over x, y_lo, core), tile: 16 (over z, y_hi).
Axes of the slice: x: 4, y: 4 (y_hi: 2, y_lo: 2; y = y_hi * 2 + y_lo), z: 8, core: 2. Of those that a mesh axis runs over, the one named last changes fastest.
Arguments:
- raw: bfloat16 [32, 1024, 4096], P(None, 'proj', 'tile'), may hold values from -6 to 6
- row_weights: bfloat16 [32, 16, 128, 256], P('proj', 'tile'), may hold values from 0 to 1
- col_weights: bfloat16 [32, 16, 1024, 2048], P('proj', 'tile'), may hold values from 0 to 1
- band_start: int32 [32, 16], replicated, may hold values from 0 to 768
- band_length: int32 [32, 16], replicated, may hold values from 64 to 256, as said below
- col_offset: int32 [32, 16], P('proj', 'tile'), may hold values from 0 to 24
Outputs:
- slab: float32 [128, 32768], P('proj', 'tile')
Inputs may be any that keep to these rules, and one draw needn't show every extreme that they name: `band_length`: in every projection some tile uses exactly 256 rows.
All inputs are finite; a program needn't handle non-finite values.
Results may differ from a plain program's by a relative error of at most 0.008.
Values may be sent and summed in bfloat16 or wider, within the bound.
No kernel may reach another device: no remote copies, remote signals or barrier semaphores. Data moves between devices by JAX's collectives and lax.ppermute only.
A program may use at most 128 MiB of HBM per device.

v0:
```python
import math
import jax
import jax.numpy as jnp
from jax import lax
from jax.sharding import PartitionSpec as P

LMAX = 256


def with_halo(array, sides, width):
    for axis, dim in sides:
        count, length = (lax.axis_size(axis), array.shape[dim])
        up = [(i, (i + 1) % count) for i in range(count - 1)]
        down = [(j, i) for i, j in up]
        last = lax.slice_in_dim(array, length - width, length, axis=dim)
        leading = lax.slice_in_dim(array, 0, width, axis=dim)
        before = lax.ppermute(last, axis, up)
        after = lax.ppermute(leading, axis, down)
        array = jnp.concatenate([before, array, after], axis=dim)
    return array


def tap_tiles():
    rows_a = jnp.arange(128, dtype=jnp.int32)[:, None]
    cols_c = jnp.arange(128, dtype=jnp.int32)[None, :]
    tiles = []
    for shift in (-1, 0, 1):
        offset = cols_c - rows_a - 128 * shift
        offset_f = offset.astype(jnp.float32)
        odd_mask = offset % 2 != 0
        safe_sq = jnp.where(offset == 0, 1.0, offset_f * offset_f)
        value = jnp.where(
            offset == 0, 0.25, jnp.where(odd_mask, -1.0 / (math.pi * math.pi * safe_sq), 0.0)
        )
        value = jnp.where((offset >= -128) & (offset <= 127), value, 0.0)
        tiles.append(value.astype(jnp.bfloat16))
    return tiles


def mask_rows(rows, length):
    mask = jnp.arange(rows.shape[0], dtype=jnp.int32)[:, None] < length
    return jnp.where(mask, rows, jnp.zeros_like(rows))


def take_band(proj_data, start, length):
    return mask_rows(lax.dynamic_slice_in_dim(proj_data, start, LMAX, 0), length)


def body(raw, row_weights, col_weights, band_start, band_length, col_offset):
    proj_count, rows_dev, cols_dev = raw.shape
    n_proj = lax.axis_size("proj")
    n_tile = lax.axis_size("tile")
    proj_me = lax.axis_index("proj")
    tile_me = lax.axis_index("tile")
    total_rows = rows_dev * n_proj
    total_cols = cols_dev * n_tile
    dist = 2.0 * total_cols
    row_ids = (proj_me * rows_dev + jnp.arange(rows_dev, dtype=jnp.int32)).astype(jnp.float32)
    col_ids = (tile_me * cols_dev + jnp.arange(cols_dev, dtype=jnp.int32)).astype(jnp.float32)
    vcoord = row_ids + 0.5 - total_rows / 2.0
    ucoord = col_ids + 0.5 - total_cols / 2.0
    weight = dist / jnp.sqrt(dist * dist + ucoord[None, :] ** 2 + vcoord[:, None] ** 2)
    weighted = (raw.astype(jnp.float32) * weight[None]).astype(jnp.bfloat16)
    padded = with_halo(weighted, (("tile", 2),), 128)
    tiles = tap_tiles()
    blocks = cols_dev // 128
    total = jnp.zeros((proj_count, rows_dev, blocks, 128), jnp.float32)
    for index in range(3):
        piece = padded[:, :, 128 * index : 128 * index + cols_dev].reshape(
            proj_count, rows_dev, blocks, 128
        )
        total = total + jnp.einsum(
            "prna,ab->prnb", piece, tiles[index], preferred_element_type=jnp.float32
        )
    filtered = total.reshape(proj_count, rows_dev, cols_dev).astype(jnp.bfloat16)
    owned = lax.all_to_all(filtered, "proj", split_axis=0, concat_axis=1, tiled=True)
    local_count = owned.shape[0]
    first_proj = proj_me * local_count
    starts = lax.dynamic_slice_in_dim(band_start, first_proj, local_count, 0)
    lengths = lax.dynamic_slice_in_dim(band_length, first_proj, local_count, 0)
    win_cols = col_weights.shape[2]
    my_offsets = col_offset[:, 0]

    def cut_window(band_rows, offset):
        return lax.dynamic_slice_in_dim(band_rows, offset * 128, win_cols, 1)

    full = lax.all_gather(owned, "tile", axis=2, tiled=True)
    my_starts = lax.dynamic_slice_in_dim(starts, tile_me, 1, 1)[:, 0]
    my_lengths = lax.dynamic_slice_in_dim(lengths, tile_me, 1, 1)[:, 0]
    bands = jax.vmap(take_band)(full, my_starts, my_lengths)
    windows = jax.vmap(cut_window)(bands, my_offsets)
    acc = jnp.zeros((row_weights.shape[2], col_weights.shape[3]), jnp.float32)
    for local in range(local_count):
        spread = jnp.dot(
            windows[local], col_weights[local, 0], preferred_element_type=jnp.float32
        ).astype(jnp.bfloat16)
        acc = acc + jnp.dot(row_weights[local, 0], spread, preferred_element_type=jnp.float32)
    return lax.psum_scatter(acc, "proj", scatter_dimension=0, tiled=True)


def solution(mesh):
    return jax.shard_map(
        body,
        mesh=mesh,
        in_specs=(
            P(None, "proj", "tile"),
            P("proj", "tile", None, None),
            P("proj", "tile", None, None),
            P(),
            P(),
            P("proj", "tile"),
        ),
        out_specs=P("proj", "tile"),
        check_vma=False,
    )
```

profile of v0, /device:TPU:16, one launch (start us, length us, event | category | flops | bytes accessed | tf_op | source)
XLA Modules:
  0.0 398.0 jit_solution(17064370836072021085)
XLA Ops:
  6.6 0.1 rsqrt_multiply_fusion
  6.7 1.6 multiply_convert_fusion
  8.2 0.3 fusion.134
  8.5 3.6 collective-permute-start
  12.1 3.8 collective-permute-start.1
  15.9 0.5 fusion.21
  16.4 20.4 %collective-permute-done = bf16[32,64,128]{2,1,0:T(8,128)(2,1)S(1)} collective-permute-done((bf16[32,64,128]{2,1,0:T(8,128)(2,1)S(1)}, bf16[32,64,128]{2,1,0:T(8,128)(2,1)S(1)}, u32[]{:S(2)}, u32[]{:S(2)}) %collective-permute-start) | collective-permute-done | bytes 524320 | tf_op jit(solution)/shard_map/ppermute | solution.py:17
  36.8 0.4 fusion.27
  37.2 0.4 fusion.24
  37.7 0.5 fusion.16
  38.2 0.2 copy.57
  38.4 21.4 %all_to_all.18 = bf16[32,64,256]{2,1,0:T(8,128)(2,1)S(1)} all-to-all(bf16[32,64,256]{2,1,0:T(8,128)(2,1)S(1)} %bitcast.91), channel_id=1, replica_groups=mesh['proj'=16,'tile'=16] {'proj'}, dimensions={0} | all-to-all | bytes 2097152 | tf_op jit(solution)/shard_map/all_to_all | solution.py:76
  59.8 1.0 copy.30
  61.0 0.8 dynamic_slice.12
  61.7 0.1 copy.39
  61.8 0.1 copy.32
  62.2 235.7 %all-gather.2.cloned.1.call-done = bf16[2,1024,4096]{2,1,0:T(8,128)(2,1)} async-done(((bf16[2,1024,256]{2,1,0:T(8,128)(2,1)}), bf16[2,1024,4096]{2,1,0:T(8,128)(2,1)}) %all-gather.2.cloned.1.call-update) | async-done | bytes 16777232 | tf_op jit(solution)/shard_map/all_gather | solution.py:87
  297.8 10.6 %while.4 = (s32[]{:T(128)}, bf16[2,1024,4096]{2,1,0:T(8,128)(2,1)}, s32[2,3]{1,0:T(2,128)S(1)}, bf16[2,256,4096]{2,1,0:T(8,128)(2,1)}) while((s32[]{:T(128)}, bf16[2,1024,4096]{2,1,0:T(8,128)(2,1)}, s32[2,3]{1,0:T(2,128)S(1)}, bf16[2,256,4096]{2,1,0:T(8,128)(2,1)}) %tuple.45), condition=%wide.while_cond.clone, body=%wide.while_body.sunk.clone | while | flops 2 | bytes 4195937 | solution.py:46
  297.8 0.6 fusion.142
  298.4 4.7 %dynamic-slice_dynamic-update-slice_fusion.6 = bf16[2,256,4096]{2,1,0:T(8,128)(2,1)} fusion(bf16[2,256,4096]{2,1,0:T(8,128)(2,1)} %get-tuple-element.138, s32[]{:T(128)} %get-tuple-element.135, bf16[2,1024,4096]{2,1,0:T(8,128)(2,1)} %get-tuple-element.140, s32[]{:T(128)} %bitcast.86, s32[]{:T(128)} %bitcast.87), kind=kLoop, calls=%fused_computation.clone.1.clone | loop fusion | bytes 4195840 | tf_op jit(solution)/shard_map/vmap()/gather
  303.1 0.6 fusion.142
  303.7 4.7 %dynamic-slice_dynamic-update-slice_fusion.6 = bf16[2,256,4096]{2,1,0:T(8,128)(2,1)} fusion(bf16[2,256,4096]{2,1,0:T(8,128)(2,1)} %get-tuple-element.138, s32[]{:T(128)} %get-tuple-element.135, bf16[2,1024,4096]{2,1,0:T(8,128)(2,1)} %get-tuple-element.140, s32[]{:T(128)} %bitcast.86, s32[]{:T(128)} %bitcast.87), kind=kLoop, calls=%fused_computation.clone.1.clone | loop fusion | bytes 4195840 | tf_op jit(solution)/shard_map/vmap()/gather
  308.4 4.5 %broadcast_select_fusion = bf16[2,256,4096]{2,1,0:T(8,128)(2,1)} fusion(bf16[2,256,4096]{2,1,0:T(8,128)(2,1)} %get-tuple-element.12, pred[2,256]{1,0:T(4,128)(4,1)S(1)} %iota_compare_fusion), kind=kLoop, calls=%fused_computation.10 | loop fusion | flops 2097152 | bytes 8389120 | tf_op jit(solution)/shard_map/vmap(jit(_where))/select_n | solution.py:42
  312.9 6.4 %while.5 = (s32[]{:T(128)}, bf16[2,256,4096]{2,1,0:T(8,128)(2,1)}, s32[2,3]{1,0:T(2,128)S(1)}, bf16[2,256,1024]{2,1,0:T(8,128)(2,1)S(1)}) while((s32[]{:T(128)}, bf16[2,256,4096]{2,1,0:T(8,128)(2,1)}, s32[2,3]{1,0:T(2,128)S(1)}, bf16[2,256,1024]{2,1,0:T(8,128)(2,1)S(1)}) %tuple.48), condition=%wide.while_cond.1.clone, body=%wide.while_body.1.sunk.clone | while | flops 2 | bytes 1048685 | solution.py:85
  312.9 0.6 fusion.143
  313.6 2.5 dynamic-slice_dynamic-update-slice_fusion.7
  316.1 0.6 fusion.143
  316.8 2.5 dynamic-slice_dynamic-update-slice_fusion.7
  319.3 3.8 fusion.14
  323.1 3.8 fusion.12
  326.9 1.3 copy.37
  328.2 63.0 %reduce-scatter.4.cloned.1.call-done = f32[8,2048]{1,0:T(8,128)} async-done(((f32[128,2048]{1,0:T(8,128)}), f32[8,2048]{1,0:T(8,128)}) %reduce-scatter.4.cloned.1.call-update) | async-done | bytes 65552 | tf_op jit(solution)/shard_map/reduce_scatter | solution.py:98
  (26 shorter events, 0.4 us)
Async XLA Ops:
  6.5 55.4 %copy-start = (s32[32,16]{0,1:T(8,128)S(1)}, s32[32,16]{0,1:T(8,128)}, u32[]{:S(2)}) copy-start(s32[32,16]{0,1:T(8,128)} %param.10) | copy-start | bytes 6148
  6.5 9.4 %copy-start.1 = (bf16[32,64,256]{2,1,0:T(8,128)(2,1)S(1)}, bf16[32,64,256]{2,1,0:T(8,128)(2,1)}, u32[]{:S(2)}) copy-start(bf16[32,64,256]{2,1,0:T(8,128)(2,1)} %param.6) | copy-start | bytes 3145732
  6.5 291.3 %all-gather.2.cloned.1.call-start = ((), (), s32[]{:S(2)}) async-start(), calls=%async_computation.2 | async-start | bytes 17825792 | tf_op jit(solution)/shard_map/all_gather | solution.py:87
  8.5 28.3 %collective-permute-start = (bf16[32,64,128]{2,1,0:T(8,128)(2,1)S(1)}, bf16[32,64,128]{2,1,0:T(8,128)(2,1)S(1)}, u32[]{:S(2)}, u32[]{:S(2)}) collective-permute-start(bf16[32,64,128]{2,1,0:T(8,128)(2,1)S(1)} %get-tuple-element.44), channel_id=1, source_target_pairs={{0,1},{1,2},{2,3},{3,4},{4,5},{5,6},{6,7},{7,8},{8,9},{9,10},{10,1... | collective-permute-start | bytes 1572872 | tf_op jit(solution)/shard_map/ppermute | solution.py:17
  12.1 24.7 %collective-permute-start.1 = (bf16[32,64,128]{2,1,0:T(8,128)(2,1)S(1)}, bf16[32,64,128]{2,1,0:T(8,128)(2,1)S(1)}, u32[]{:S(2)}, u32[]{:S(2)}) collective-permute-start(bf16[32,64,128]{2,1,0:T(8,128)(2,1)S(1)} %get-tuple-element.43), channel_id=1, source_target_pairs={{1,0},{2,1},{3,2},{4,3},{5,4},{6,5},{7,6},{8,7},{9,8},{10,9},{11,1... | collective-permute-start | bytes 1572872 | tf_op jit(solution)/shard_map/ppermute | solution.py:18
  38.2 23.6 %copy-start.3 = (s32[2,1]{0,1:T(1,128)S(1)}, s32[2,1]{0,1:T(1,128)}, u32[]{:S(2)}) copy-start(s32[2,1]{0,1:T(1,128)} %param.11) | copy-start | bytes 28
  60.9 330.3 %reduce-scatter.4.cloned.1.call-start = ((), (), s32[]{:S(2)}) async-start(), calls=%async_computation.3 | async-start | bytes 1114112 | tf_op jit(solution)/shard_map/reduce_scatter | solution.py:98
  312.9 6.4 %copy-start.2 = (bf16[2,1,128,256]{3,2,1,0:T(8,128)(2,1)S(1)}, bf16[2,1,128,256]{3,2,1,0:T(8,128)(2,1)}, u32[]{:S(2)}) copy-start(bf16[2,1,128,256]{3,2,1,0:T(8,128)(2,1)} %param.7) | copy-start | bytes 393220
Sparse Core Ops, SparseCore 0:
  61.0 236.7 all-gather.1
  328.4 62.7 reduce-scatter.3
where the time goes:
time: 399 us; the launch traced here: 398 us
  waiting for transfers between devices  319 us (80%)
  blocking collectives  21.4 us (5%)
  local copies, waits for them, and re-layouts  20.8 us (5%)
  between operations  13.6 us (3%)
  matrix products  9.01 us (2%)
  starting transfers between devices  7.42 us (2%)
  other arithmetic  6.68 us (2%)
    all_gather x1, waiting for transfers between devices, body(): full = lax.all_gather(owned, 'tile', axis=2, tiled=True)  236 us
    reduce_scatter x1, waiting for transfers between devices, body(): return lax.psum_scatter(acc, 'proj', scatter_dimension=0, tiled=True)  63 us
    all_to_all x1, blocking collectives, body(): lax.all_to_all(filtered, 'proj', split_axis=0, concat_axis=1, tiled=True)  21.4 us
    ppermute x1, waiting for transfers between devices, with_halo(): before = lax.ppermute(last, axis, up)  20.4 us
    gather x12, local copies, waits for them, and re-layouts  16.9 us
  transfers between devices with their start and end apart: 4, of which 3 were waited for; matrix products, arithmetic and copies ran while one was open for 0% of the time, Pallas kernels for 0%

commit v1 on v0

--- a/solution.py
+++ b/solution.py
@@ -84,7 +84,9 @@
     def cut_window(band_rows, offset):
         return lax.dynamic_slice_in_dim(band_rows, offset * 128, win_cols, 1)
 
-    full = lax.all_gather(owned, "tile", axis=2, tiled=True)
+    full = jnp.concatenate(
+        lax.all_to_all(jnp.stack([owned] * lax.axis_size("tile")), "tile", 0, 0), axis=2
+    )
     my_starts = lax.dynamic_slice_in_dim(starts, tile_me, 1, 1)[:, 0]
     my_lengths = lax.dynamic_slice_in_dim(lengths, tile_me, 1, 1)[:, 0]
     bands = jax.vmap(take_band)(full, my_starts, my_lengths)

time: 399 us -> 594 us (1.49)
  waiting for transfers between devices: 319 us -> 462 us
  local copies, waits for them, and re-layouts: 20.8 us -> 58.8 us
  starting transfers between devices: 7.42 us -> 19.9 us
    all_to_all x0 -> x1, waiting for transfers between devices: none -> 381 us  [body(): lax.all_to_all(jnp.stack([owned] * lax.axis_size('tile')), 'tile', 0, 0)]
    all_gather x1 -> x0, waiting for transfers between devices: 236 us -> none  [body(): full = lax.all_gather(owned, 'tile', axis=2, tiled=True)]
    all_to_all x0 -> x1, local copies, waits for them, and re-layouts: none -> 22.4 us  [body(): lax.all_to_all(jnp.stack([owned] * lax.axis_size('tile')), 'tile', 0, 0)]
    all_to_all x0 -> x1, starting transfers between devices: none -> 11.6 us  [body(): lax.all_to_all(jnp.stack([owned] * lax.axis_size('tile')), 'tile', 0, 0)]
    gather x12 -> x16, local copies, waits for them, and re-layouts: 16.9 us -> 27.4 us
    ppermute x1, waiting for transfers between devices: 0.01 us -> 9.31 us  [with_halo(): after = lax.ppermute(leading, axis, down)]
    ppermute x1, waiting for transfers between devices: 20.4 us -> 11.1 us  [with_halo(): before = lax.ppermute(last, axis, up)]
    another operation x0 -> x1, local copies, waits for them, and re-layouts: none -> 5.94 us  [body(): jnp.stack([owned] * lax.axis_size('tile'))]
  transfers between devices with their start and end apart: 4 -> 4, of which waited for: 3 -> 4; matrix products, arithmetic and copies ran while one was open for 0% -> 0% of each run, Pallas kernels for 0% -> 0%
where the time goes in v1:
time: 594 us; the launch traced here: 593 us
  waiting for transfers between devices  462 us (78%)
  local copies, waits for them, and re-layouts  58.8 us (10%)
  blocking collectives  21.4 us (4%)
  starting transfers between devices  19.9 us (3%)
  between operations  13.5 us (2%)
  matrix products  10.3 us (2%)
  other arithmetic  6.7 us (1%)
    all_to_all x1, waiting for transfers between devices, body(): lax.all_to_all(jnp.stack([owned] * lax.axis_size('tile')), 'tile', 0, 0)  381 us
    reduce_scatter x1, waiting for transfers between devices, body(): return lax.psum_scatter(acc, 'proj', scatter_dimension=0, tiled=True)  60.8 us
    gather x16, local copies, waits for them, and re-layouts  27.4 us
    all_to_all x1, local copies, waits for them, and re-layouts, body(): lax.all_to_all(jnp.stack([owned] * lax.axis_size('tile')), 'tile', 0, 0)  22.4 us
    all_to_all x1, blocking collectives, body(): lax.all_to_all(filtered, 'proj', split_axis=0, concat_axis=1, tiled=True)  21.4 us
  transfers between devices with their start and end apart: 4, of which 4 were waited for; matrix products, arithmetic and copies ran while one was open for 0% of the time, Pallas kernels for 0%

profile of v1, /device:TPU:16, one launch (start us, length us, event | category | flops | bytes accessed | tf_op | source)
XLA Modules:
  0.0 592.7 jit_solution(11277636174936657185)
XLA Ops:
  6.7 1.6 multiply_convert_fusion
  8.5 4.0 collective-permute-start.1
  12.5 4.3 collective-permute-start
  16.8 0.5 fusion.21
  17.3 9.3 %collective-permute-done.1 = bf16[32,64,128]{2,1,0:T(8,128)(2,1)S(1)} collective-permute-done((bf16[32,64,128]{2,1,0:T(8,128)(2,1)S(1)}, bf16[32,64,128]{2,1,0:T(8,128)(2,1)S(1)}, u32[]{:S(2)}, u32[]{:S(2)}) %collective-permute-start.1) | collective-permute-done | bytes 524320 | tf_op jit(solution)/shard_map/ppermute | solution.py:18
  26.6 11.1 %collective-permute-done = bf16[32,64,128]{2,1,0:T(8,128)(2,1)S(1)} collective-permute-done((bf16[32,64,128]{2,1,0:T(8,128)(2,1)S(1)}, bf16[32,64,128]{2,1,0:T(8,128)(2,1)S(1)}, u32[]{:S(2)}, u32[]{:S(2)}) %collective-permute-start) | collective-permute-done | bytes 524320 | tf_op jit(solution)/shard_map/ppermute | solution.py:17
  38.6 0.5 fusion.16
  39.3 21.4 %all_to_all.20 = bf16[32,64,256]{2,1,0:T(8,128)(2,1)S(1)} all-to-all(bf16[32,64,256]{2,1,0:T(8,128)(2,1)S(1)} %bitcast.95), channel_id=1, replica_groups=mesh['proj'=16,'tile'=16] {'proj'}, dimensions={0} | all-to-all | bytes 2097152 | tf_op jit(solution)/shard_map/all_to_all | solution.py:76
  60.8 5.9 %stack.5 = bf16[16,2,1024,256]{3,2,1,0:T(8,128)(2,1)} broadcast(bf16[2,1024,256]{2,1,0:T(8,128)(2,1)S(1)} %bitcast.94), dimensions={1,2,3} | broadcast | bytes 17825792 | tf_op jit(solution)/shard_map/stack | solution.py:88
  66.7 11.6 %all-to-all-start.1 = ((bf16[16,2,1024,256]{3,2,1,0:T(8,128)(2,1)}), bf16[16,2,1024,256]{3,2,1,0:T(8,128)(2,1)}, u32[]{:S(2)}, u32[]{:S(2)}) async-start(bf16[16,2,1024,256]{3,2,1,0:T(8,128)(2,1)} %stack.5), calls=%async_computation.1 | async-start | bytes 33554432 | tf_op jit(solution)/shard_map/all_to_all | solution.py:88
  78.5 0.8 dynamic_slice.12
  79.6 380.9 %all-to-all-done.1 = bf16[16,2,1024,256]{3,2,1,0:T(8,128)(2,1)} async-done(((bf16[16,2,1024,256]{3,2,1,0:T(8,128)(2,1)}), bf16[16,2,1024,256]{3,2,1,0:T(8,128)(2,1)}, u32[]{:S(2)}, u32[]{:S(2)}) %all-to-all-start.1) | async-done | bytes 16777248 | tf_op jit(solution)/shard_map/all_to_all | solution.py:88
  460.5 22.4 %copy.39 = bf16[16,2,1024,256]{2,3,0,1:T(8,128)(2,1)} copy(bf16[16,2,1024,256]{3,2,1,0:T(8,128)(2,1)} %all-to-all-done.1) | data formatting | bytes 33554432 | tf_op jit(solution)/shard_map/all_to_all | solution.py:88
  482.9 21.1 %while.4 = (s32[]{:T(128)}, bf16[2,1024,4096]{1,2,0:T(8,128)(2,1)}, s32[2,3]{1,0:T(2,128)S(1)}, bf16[2,256,4096]{2,1,0:T(8,128)(2,1)}) while((s32[]{:T(128)}, bf16[2,1024,4096]{1,2,0:T(8,128)(2,1)}, s32[2,3]{1,0:T(2,128)S(1)}, bf16[2,256,4096]{2,1,0:T(8,128)(2,1)}) %tuple.54), condition=%wide.while_cond.clone, body=%wide.while_body.sunk.clone | while | flops 2 | bytes 12583029 | solution.py:46
  482.9 0.6 fusion.142
  483.5 5.5 constant_dynamic-slice_fusion.10
  489.1 2.9 copy.71
  492.0 1.4 constant_dynamic-update-slice_fusion.3
  493.4 0.6 fusion.142
  494.0 5.5 constant_dynamic-slice_fusion.10
  499.6 2.9 copy.71
  502.5 1.5 constant_dynamic-update-slice_fusion.3
  504.0 4.5 broadcast_select_fusion
  508.5 6.4 %while.5 = (s32[]{:T(128)}, bf16[2,256,4096]{2,1,0:T(8,128)(2,1)}, s32[2,3]{1,0:T(2,128)S(1)}, bf16[2,256,1024]{2,1,0:T(8,128)(2,1)S(1)}) while((s32[]{:T(128)}, bf16[2,256,4096]{2,1,0:T(8,128)(2,1)}, s32[2,3]{1,0:T(2,128)S(1)}, bf16[2,256,1024]{2,1,0:T(8,128)(2,1)S(1)}) %tuple.49), condition=%wide.while_cond.1.clone, body=%wide.while_body.1.sunk.clone | while | flops 2 | bytes 1048693 | solution.py:85
  508.5 0.6 fusion.143
  509.2 2.5 dynamic-slice_dynamic-update-slice_fusion.3
  511.7 0.6 fusion.143
  512.4 2.5 dynamic-slice_dynamic-update-slice_fusion.3
  514.9 4.7 fusion.14
  519.7 4.1 fusion.12
  523.7 1.3 copy.47
  525.1 60.8 %reduce-scatter.4.cloned.1.call-done = f32[8,2048]{1,0:T(8,128)} async-done(((f32[128,2048]{1,0:T(8,128)}), f32[8,2048]{1,0:T(8,128)}) %reduce-scatter.4.cloned.1.call-update) | async-done | bytes 65552 | tf_op jit(solution)/shard_map/reduce_scatter | solution.py:100
  (33 shorter events, 2.0 us)
Async XLA Ops:
  6.5 72.8 %copy-start = (s32[32,16]{0,1:T(8,128)S(1)}, s32[32,16]{0,1:T(8,128)}, u32[]{:S(2)}) copy-start(s32[32,16]{0,1:T(8,128)} %param.10) | copy-start | bytes 6148
  6.6 10.2 %copy-start.2 = (bf16[32,64,256]{2,1,0:T(8,128)(2,1)S(1)}, bf16[32,64,256]{2,1,0:T(8,128)(2,1)}, u32[]{:S(2)}) copy-start(bf16[32,64,256]{2,1,0:T(8,128)(2,1)} %param.6) | copy-start | bytes 3145732
  8.5 18.1 %collective-permute-start.1 = (bf16[32,64,128]{2,1,0:T(8,128)(2,1)S(1)}, bf16[32,64,128]{2,1,0:T(8,128)(2,1)S(1)}, u32[]{:S(2)}, u32[]{:S(2)}) collective-permute-start(bf16[32,64,128]{2,1,0:T(8,128)(2,1)S(1)} %get-tuple-element.47), channel_id=1, source_target_pairs={{1,0},{2,1},{3,2},{4,3},{5,4},{6,5},{7,6},{8,7},{9,8},{10,9},{11,1... | collective-permute-start | bytes 1572872 | tf_op jit(solution)/shard_map/ppermute | solution.py:18
  12.5 25.2 %collective-permute-start = (bf16[32,64,128]{2,1,0:T(8,128)(2,1)S(1)}, bf16[32,64,128]{2,1,0:T(8,128)(2,1)S(1)}, u32[]{:S(2)}, u32[]{:S(2)}) collective-permute-start(bf16[32,64,128]{2,1,0:T(8,128)(2,1)S(1)} %get-tuple-element.48), channel_id=1, source_target_pairs={{0,1},{1,2},{2,3},{3,4},{4,5},{5,6},{6,7},{7,8},{8,9},{9,10},{10,1... | collective-permute-start | bytes 1572872 | tf_op jit(solution)/shard_map/ppermute | solution.py:17
  66.7 11.7 %copy-start.4 = (s32[2,1]{0,1:T(1,128)S(1)}, s32[2,1]{0,1:T(1,128)}, u32[]{:S(2)}) copy-start(s32[2,1]{0,1:T(1,128)} %param.11) | copy-start | bytes 28
  66.7 393.7 %all-to-all-start.1 = ((bf16[16,2,1024,256]{3,2,1,0:T(8,128)(2,1)}), bf16[16,2,1024,256]{3,2,1,0:T(8,128)(2,1)}, u32[]{:S(2)}, u32[]{:S(2)}) async-start(bf16[16,2,1024,256]{3,2,1,0:T(8,128)(2,1)} %stack.5), calls=%async_computation.1 | async-start | bytes 33554432 | tf_op jit(solution)/shard_map/all_to_all | solution.py:88
  78.3 507.6 %reduce-scatter.4.cloned.1.call-start = ((), (), s32[]{:S(2)}) async-start(), calls=%async_computation.3 | async-start | bytes 1114112 | tf_op jit(solution)/shard_map/reduce_scatter | solution.py:100
  508.5 6.4 %copy-start.3 = (bf16[2,1,128,256]{3,2,1,0:T(8,128)(2,1)S(1)}, bf16[2,1,128,256]{3,2,1,0:T(8,128)(2,1)}, u32[]{:S(2)}) copy-start(bf16[2,1,128,256]{3,2,1,0:T(8,128)(2,1)} %param.7) | copy-start | bytes 393220
  519.7 66.2 %copy-start.1 = (s32[32,16]{0,1:T(8,128)S(1)}, s32[32,16]{0,1:T(8,128)}, u32[]{:S(2)}) copy-start(s32[32,16]{0,1:T(8,128)} %param.10) | copy-start | bytes 6148
Sparse Core Ops, SparseCore 0:
  525.2 60.6 reduce-scatter.3
